TPU v7x, 32 devices: a whole 2x2x4 slice. The times are simulated.
32 devices in a mesh: section: 2 (over y), dp: 4 (over x, core), tensor: 4 (over z).
Axes of the slice: x: 2, y: 2, z: 4, core: 2. Of those that a mesh axis runs over, the one named last changes fastest.
Arguments:
- master_weight: float32 [2304, 128, 128], P(('section', 'tensor'), 'dp'), parts along dimension 0, may hold values from -6 to 6
- first_moment: float32 [2304, 128, 128], P(('section', 'tensor'), 'dp'), parts along dimension 0, may hold values from -2 to 2
- second_moment: float32 [2304, 128, 128], P(('section', 'tensor'), 'dp'), parts along dimension 0, may hold values from 0.01 to 1
- grads: bfloat16 [4, 2304, 128, 128], P('dp', ('section', 'tensor')), parts along dimension 1, may hold values from -6 to 6
- dest_table: int32 [1152], replicated, may hold values from 0 to 1151, as said below
Outputs:
- weight_new: float32 [2304, 128, 128], P(('section', 'tensor'), 'dp'), parts along dimension 0
- first_new: float32 [2304, 128, 128], P(('section', 'tensor'), 'dp'), parts along dimension 0
- second_new: float32 [2304, 128, 128], P(('section', 'tensor'), 'dp'), parts along dimension 0
- weights: bfloat16 [2304, 128, 128], P(('section', 'tensor')), parts along dimension 0
There are 2 independent parts, one for each index of `section`. A program takes and returns all parts, laid end to end along the dimension named above; an argument that names none is the same for every part. Nothing has to cross between parts.
Inputs may be any that keep to these rules, and one draw needn't show every extreme that they name: `dest_table`: A permutation. Group old slots by s // 288 and new positions by p // 288: at most 72 slots of one group have positions in one block, and some pair of group and block has exactly 72.
All inputs are finite; a program needn't handle non-finite values.
Results may differ from a plain program's by a relative error of at most 0.0023.
Values may be sent and summed in bfloat16 or wider, within the bound.
A program may use at most 128 MiB of HBM per device.

v0:
```python
import jax
import jax.numpy as jnp
from jax import lax
from jax.sharding import PartitionSpec as P

STEP = 10


learn_rate = 0.04
decay_rate = 1.5
beta_first = 0.9
beta_second = 0.95
epsilon = 1e-08


def adam_step(weight, first, second, grad):
    first_new = beta_first * first + (1.0 - beta_first) * grad
    second_new = beta_second * second + (1.0 - beta_second) * grad * grad
    first_hat = first_new / (1.0 - beta_first**STEP)
    second_hat = second_new / (1.0 - beta_second**STEP)
    weight_new = weight - learn_rate * (
        first_hat / (jnp.sqrt(second_hat) + epsilon) + decay_rate * weight
    )
    return (weight_new, first_new, second_new)


def routes(dest_table, slots, groups, capacity, rank_here):
    total = dest_table.shape[0]
    source = jnp.arange(total, dtype=jnp.int32) // slots
    target = dest_table // slots
    local = dest_table % slots
    layout = target.reshape(groups, slots)
    marks = (layout[:, :, None] == jnp.arange(groups, dtype=jnp.int32)[None, None, :]).astype(
        jnp.int32
    )
    running = jnp.cumsum(marks, axis=1)
    within = (jnp.sum(marks * running, axis=2) - 1).reshape(total)
    outgoing = lax.dynamic_slice_in_dim(target * capacity + within, rank_here * slots, slots)
    landing = jnp.where(target == rank_here, local, slots)
    incoming = (
        jnp.zeros((slots,), jnp.int32).at[landing].set(source * capacity + within, mode="drop")
    )
    return (outgoing, incoming)


def packed(values, index, length):
    empty = jnp.zeros((length,) + values.shape[1:], values.dtype)
    return empty.at[index].set(values)


def shards(master_weight, first_moment, second_moment, grads, dest_table):
    groups = lax.axis_size("tensor")
    rank_here = lax.axis_index("tensor")
    slots = master_weight.shape[0]
    capacity = 2 * ((slots + 2 * groups - 1) // (2 * groups))
    length = groups * capacity
    outgoing, incoming = routes(dest_table, slots, groups, capacity, rank_here)
    replicas = lax.axis_size("dp")
    summed = lax.psum_scatter(
        grads[0].astype(jnp.float32).astype(jnp.bfloat16), "dp", scatter_dimension=1, tiled=True
    ).astype(jnp.float32)
    grad = summed / replicas
    moved = (
        lax.all_to_all(
            packed(master_weight, outgoing, length),
            "tensor",
            split_axis=0,
            concat_axis=0,
            tiled=True,
        ),
        lax.all_to_all(
            packed(first_moment, outgoing, length),
            "tensor",
            split_axis=0,
            concat_axis=0,
            tiled=True,
        ),
        lax.all_to_all(
            packed(second_moment, outgoing, length),
            "tensor",
            split_axis=0,
            concat_axis=0,
            tiled=True,
        ),
    )
    weight_new, first_new, second_new = adam_step(
        moved[0][incoming], moved[1][incoming], moved[2][incoming], grad
    )
    weights = lax.all_gather(weight_new.astype(jnp.bfloat16), "dp", axis=1, tiled=True)
    return (weight_new, first_new, second_new, weights)


def solution(mesh):
    placed = (
        P(("section", "tensor"), "dp", None),
        P(("section", "tensor"), "dp", None),
        P(("section", "tensor"), "dp", None),
        P("dp", ("section", "tensor"), None, None),
        P(),
    )
    return jax.shard_map(
        shards,
        mesh=mesh,
        in_specs=placed,
        out_specs=(
            P(("section", "tensor"), "dp", None),
            P(("section", "tensor"), "dp", None),
            P(("section", "tensor"), "dp", None),
            P(("section", "tensor"), None, None),
        ),
        check_vma=False,
    )
```

profile of v0, /device:TPU:9, one launch (start us, length us, event | category | flops | bytes accessed | tf_op | source)
XLA Modules:
  0.0 482.0 jit_solution(14738658878361883236)
XLA Ops:
  7.2 0.7 compare_select_fusion
  7.9 0.1 eq.30
  8.0 4.8 %reduce-window.6 = s32[4,4,3,128]{3,2,1,0:T(4,128)S(1)} reduce-window(s32[4,4,3,128]{3,2,1,0:T(4,128)S(1)} %copy.11, s32[]{:T(128)} %constant.32.clone.1), window={size=1x1x1x128 pad=0_0x0_0x0_0x127_0}, to_apply=%region_0.1 | reduce-window | flops 780288 | bytes 49156 | tf_op jit(solution)/shard_map/reduce-window
  12.9 0.1 slice.18
  12.9 0.2 copy.12
  13.1 0.1 copy.13
  13.2 0.1 broadcast_add_fusion
  13.4 0.1 sub.21
  13.5 0.1 compare_select_fusion.2
  13.5 2.8 broadcast.40.clone.1
  16.3 38.9 %scatter_fusion.1 = f32[288,32,128]{2,1,0:T(8,128)} fusion(f32[288,32,128]{2,1,0:T(8,128)} %broadcast.40.clone.1, s32[288]{0:T(512)S(1)} %compare_select_fusion.2, f32[288,32,128]{2,1,0:T(8,128)} %param.6), kind=kCustom, calls=%fused_computation.5 | custom fusion | bytes 14156928 | tf_op jit(solution)/shard_map/scatter | solution.py:48
  55.3 5.0 %all-to-all-start.1 = ((f32[288,32,128]{2,1,0:T(8,128)}), f32[288,32,128]{2,1,0:T(8,128)}, u32[]{:S(2)}, u32[]{:S(2)}) async-start(f32[288,32,128]{2,1,0:T(8,128)} %scatter_fusion.1), calls=%async_computation.1 | async-start | bytes 9437184 | tf_op jit(solution)/shard_map/all_to_all | solution.py:71
  60.2 0.0 reduce-scatter.2.cloned.1.call-start
  60.3 0.7 reduce-scatter.2.cloned.1.call-update
  61.0 2.8 broadcast.40.clone
  63.8 39.8 %scatter_fusion = f32[288,32,128]{2,1,0:T(8,128)} fusion(f32[288,32,128]{2,1,0:T(8,128)} %broadcast.40.clone, s32[288]{0:T(512)S(1)} %compare_select_fusion.2, f32[288,32,128]{2,1,0:T(8,128)} %param.5), kind=kCustom, calls=%fused_computation.3 | custom fusion | bytes 14156928 | tf_op jit(solution)/shard_map/scatter | solution.py:48
  103.6 57.3 %all-to-all-done.1 = f32[288,32,128]{2,1,0:T(8,128)} async-done(((f32[288,32,128]{2,1,0:T(8,128)}), f32[288,32,128]{2,1,0:T(8,128)}, u32[]{:S(2)}, u32[]{:S(2)}) %all-to-all-start.1) | async-done | bytes 4718624 | tf_op jit(solution)/shard_map/all_to_all | solution.py:71
  160.9 8.3 %all-to-all-start = ((f32[288,32,128]{2,1,0:T(8,128)}), f32[288,32,128]{2,1,0:T(8,128)}, u32[]{:S(2)}, u32[]{:S(2)}) async-start(f32[288,32,128]{2,1,0:T(8,128)} %scatter_fusion), calls=%async_computation | async-start | bytes 9437184 | tf_op jit(solution)/shard_map/all_to_all | solution.py:64
  169.2 2.8 broadcast.40.clone.2
  172.0 38.9 %scatter_fusion.2 = f32[288,32,128]{2,1,0:T(8,128)} fusion(f32[288,32,128]{2,1,0:T(8,128)} %broadcast.40.clone.2, s32[288]{0:T(512)S(1)} %compare_select_fusion.2, f32[288,32,128]{2,1,0:T(8,128)} %param.7), kind=kCustom, calls=%fused_computation.6 | custom fusion | bytes 14156928 | tf_op jit(solution)/shard_map/scatter | solution.py:48
  210.9 58.3 %all-to-all-done = f32[288,32,128]{2,1,0:T(8,128)} async-done(((f32[288,32,128]{2,1,0:T(8,128)}), f32[288,32,128]{2,1,0:T(8,128)}, u32[]{:S(2)}, u32[]{:S(2)}) %all-to-all-start) | async-done | bytes 4718624 | tf_op jit(solution)/shard_map/all_to_all | solution.py:64
  269.2 8.9 %all-to-all-start.2 = ((f32[288,32,128]{2,1,0:T(8,128)}), f32[288,32,128]{2,1,0:T(8,128)}, u32[]{:S(2)}, u32[]{:S(2)}) async-start(f32[288,32,128]{2,1,0:T(8,128)} %scatter_fusion.2), calls=%async_computation.3 | async-start | bytes 9437184 | tf_op jit(solution)/shard_map/all_to_all | solution.py:78
  278.1 0.0 all-gather.2.cloned.1.call-start
  278.1 6.4 %scatter_custom_fusion.1 = s32[288]{0:T(512)S(1)} fusion(s32[1152]{0:T(1024)S(1)} %get-tuple-element.8, s32[1152]{0:T(1024)S(1)} %fusion.5, s32[]{:T(128)} %constant.32.clone.1), kind=kCustom, calls=%fused_computation.44 | custom fusion | bytes 1156 | tf_op jit(solution)/shard_map/scatter | solution.py:41
  284.6 5.4 %gather_fusion.1 = f32[288,32,128]{2,1,0:T(8,128)} fusion(f32[288,32,128]{2,1,0:T(8,128)} %all-to-all-done.1, s32[1024]{0:T(1024)S(1)} %pad_clamp_fusion), kind=kCustom, calls=%fused_computation.1 | custom fusion | bytes 9438336 | tf_op jit(solution)/shard_map/gather | solution.py:87
  290.0 5.4 %gather_fusion = f32[288,32,128]{2,1,0:T(8,128)} fusion(f32[288,32,128]{2,1,0:T(8,128)} %all-to-all-done, s32[1024]{0:T(1024)S(1)} %pad_clamp_fusion), kind=kCustom, calls=%fused_computation | custom fusion | bytes 9438336 | tf_op jit(solution)/shard_map/gather | solution.py:87
  295.4 82.8 %all-to-all-done.2 = f32[288,32,128]{2,1,0:T(8,128)} async-done(((f32[288,32,128]{2,1,0:T(8,128)}), f32[288,32,128]{2,1,0:T(8,128)}, u32[]{:S(2)}, u32[]{:S(2)}) %all-to-all-start.2) | async-done | bytes 4718624 | tf_op jit(solution)/shard_map/all_to_all | solution.py:78
  378.2 5.4 %gather_fusion.2 = f32[288,32,128]{2,1,0:T(8,128)} fusion(f32[288,32,128]{2,1,0:T(8,128)} %all-to-all-done.2, s32[1024]{0:T(1024)S(1)} %pad_clamp_fusion), kind=kCustom, calls=%fused_computation.2 | custom fusion | bytes 9438336 | tf_op jit(solution)/shard_map/gather | solution.py:87
  383.6 0.0 reduce-scatter.2.cloned.1.call-done
  383.6 11.5 %fusion.15 = (bf16[288,32,128]{2,1,0:T(8,128)(2,1)}, f32[288,32,128]{2,1,0:T(8,128)}, f32[288,32,128]{2,1,0:T(8,128)}, f32[288,32,128]{2,1,0:T(8,128)}) fusion(f32[288,32,128]{2,1,0:T(8,128)} %gather_fusion, bf16[288,32,128]{2,1,0:T(8,128)(2,1)} %reduce-scatter.2.cloned.1.call-done, f32[288,32,128]{2,1,0:T(8,128)} %gather_fusion.1, ...), kind=kLoop, calls=%fused_computation.46 | loop fusion | flops 21233664 | bytes 33030144 | tf_op jit(solution)/shard_map/convert_element_type | solution.py:89
  395.1 0.0 all-gather.2.cloned.1.call-update
  395.1 68.4 %all-gather.2.cloned.1.call-done = bf16[288,128,128]{2,1,0:T(8,128)(2,1)} async-done(((bf16[288,32,128]{2,1,0:T(8,128)(2,1)}), bf16[288,128,128]{2,1,0:T(8,128)(2,1)}) %all-gather.2.cloned.1.call-update) | async-done | bytes 9437200 | tf_op jit(solution)/shard_map/all_gather | solution.py:89
  463.5 11.7 %copy.18 = bf16[288,128,128]{2,1,0:T(8,128)(2,1)} copy(bf16[288,128,128]{2,1,0:T(8,128)(2,1)} %all-gather.2.cloned.1.call-done) | data formatting | bytes 18874368
  (11 shorter events, 0.1 us)
Async XLA Ops:
  55.3 105.6 %all-to-all-start.1 = ((f32[288,32,128]{2,1,0:T(8,128)}), f32[288,32,128]{2,1,0:T(8,128)}, u32[]{:S(2)}, u32[]{:S(2)}) async-start(f32[288,32,128]{2,1,0:T(8,128)} %scatter_fusion.1), calls=%async_computation.1 | async-start | bytes 9437184 | tf_op jit(solution)/shard_map/all_to_all | solution.py:71
  60.2 323.3 %reduce-scatter.2.cloned.1.call-start = ((), (), s32[]{:S(2)}) async-start(), calls=%async_computation.4 | async-start | bytes 11796480 | tf_op jit(solution)/shard_map/reduce_scatter | solution.py:59
  160.9 108.3 %all-to-all-start = ((f32[288,32,128]{2,1,0:T(8,128)}), f32[288,32,128]{2,1,0:T(8,128)}, u32[]{:S(2)}, u32[]{:S(2)}) async-start(f32[288,32,128]{2,1,0:T(8,128)} %scatter_fusion), calls=%async_computation | async-start | bytes 9437184 | tf_op jit(solution)/shard_map/all_to_all | solution.py:64
  269.2 109.0 %all-to-all-start.2 = ((f32[288,32,128]{2,1,0:T(8,128)}), f32[288,32,128]{2,1,0:T(8,128)}, u32[]{:S(2)}, u32[]{:S(2)}) async-start(f32[288,32,128]{2,1,0:T(8,128)} %scatter_fusion.2), calls=%async_computation.3 | async-start | bytes 9437184 | tf_op jit(solution)/shard_map/all_to_all | solution.py:78
  278.1 185.4 %all-gather.2.cloned.1.call-start = ((), (), s32[]{:S(2)}) async-start(), calls=%async_computation.5 | async-start | bytes 11796480 | tf_op jit(solution)/shard_map/all_gather | solution.py:89
Sparse Core Ops, SparseCore 0:
  63.6 78.8 reduce-scatter.1
  395.2 68.2 all-gather.1
where the time goes:
time: 485 us; the launch traced here: 482 us
  waiting for transfers between devices  268 us (55%)
  local copies, waits for them, and re-layouts  161 us (33%)
  starting transfers between devices  22.2 us (5%)
  other arithmetic  17.3 us (4%)
  between operations  14.1 us (3%)
    scatter x3, local copies, waits for them, and re-layouts, packed(): return empty.at[index].set(values)  118 us
    all_to_all x1, waiting for transfers between devices, shards(): lax.all_to_all(packed(second_moment, outgoing, length), 'tensor', split_a...  82.8 us
    all_gather x1, waiting for transfers between devices, shards(): lax.all_gather(weight_new.astype(jnp.bfloat16), 'dp', axis=1, tiled=True)  68.4 us
    all_to_all x1, waiting for transfers between devices, shards(): lax.all_to_all(packed(master_weight, outgoing, length), 'tensor', split_a...  58.3 us
    all_to_all x1, waiting for transfers between devices, shards(): lax.all_to_all(packed(first_moment, outgoing, length), 'tensor', split_ax...  57.3 us
    unnamed x1, local copies, waits for them, and re-layouts  11.7 us
    convert_element_type x1, other arithmetic, shards(): weight_new.astype(jnp.bfloat16)  11.5 us
  transfers between devices with their start and end apart: 5, of which 4 were waited for; matrix products, arithmetic and copies ran while one was open for 22% of the time, Pallas kernels for 0%

commit v1 on v0

v1 whole, which is shorter than its diff:
```python
import jax
import jax.numpy as jnp
from jax import lax
from jax.sharding import PartitionSpec as P

STEP = 10


learn_rate = 0.04
decay_rate = 1.5
beta_first = 0.9
beta_second = 0.95
epsilon = 1e-08


def adam_step(weight, first, second, grad):
    first_new = beta_first * first + (1.0 - beta_first) * grad
    second_new = beta_second * second + (1.0 - beta_second) * grad * grad
    first_hat = first_new / (1.0 - beta_first**STEP)
    second_hat = second_new / (1.0 - beta_second**STEP)
    weight_new = weight - learn_rate * (
        first_hat / (jnp.sqrt(second_hat) + epsilon) + decay_rate * weight
    )
    return (weight_new, first_new, second_new)


def routes(dest_table, slots, groups, capacity, rank_here):
    total = dest_table.shape[0]
    length = groups * capacity
    target = dest_table // slots
    local = dest_table % slots
    layout = target.reshape(groups, slots)
    order = jnp.arange(slots, dtype=jnp.int32)
    same = (layout[:, :, None] == layout[:, None, :]) & (order[None, :] < order[:, None])[None]
    within = jnp.sum(same.astype(jnp.int32), axis=2).reshape(total)
    source = jnp.arange(total, dtype=jnp.int32) // slots
    leaving = lax.dynamic_slice_in_dim(target * capacity + within, rank_here * slots, slots)
    places = jnp.arange(length, dtype=jnp.int32)
    outgoing = jnp.sum(jnp.where(leaving[None, :] == places[:, None], order[None, :], 0), axis=1)
    landing = jnp.where(target == rank_here, local, slots)
    incoming = jnp.sum(
        jnp.where(landing[None, :] == order[:, None], (source * capacity + within)[None, :], 0),
        axis=1,
    )
    return (outgoing, incoming)


def take(values, index):
    return values.at[index].get(mode="promise_in_bounds")


def shards(master_weight, first_moment, second_moment, grads, dest_table):
    groups = lax.axis_size("tensor")
    rank_here = lax.axis_index("tensor")
    slots = master_weight.shape[0]
    capacity = 2 * ((slots + 2 * groups - 1) // (2 * groups))
    outgoing, incoming = routes(dest_table, slots, groups, capacity, rank_here)
    replicas = lax.axis_size("dp")
    summed = lax.psum_scatter(grads[0], "dp", scatter_dimension=1, tiled=True).astype(jnp.float32)
    grad = summed / replicas

    def move(values):
        return lax.all_to_all(values, "tensor", split_axis=0, concat_axis=0, tiled=True)

    weight = move(take(master_weight, outgoing))
    first = move(take(first_moment, outgoing).astype(jnp.bfloat16))
    second = move(take(second_moment, outgoing).astype(jnp.bfloat16))
    weight_new, first_new, second_new = adam_step(
        take(weight, incoming),
        take(first, incoming).astype(jnp.float32),
        take(second, incoming).astype(jnp.float32),
        grad,
    )
    weights = lax.all_gather(weight_new.astype(jnp.bfloat16), "dp", axis=1, tiled=True)
    return (weight_new, first_new, second_new, weights)


def solution(mesh):
    placed = (
        P(("section", "tensor"), "dp", None),
        P(("section", "tensor"), "dp", None),
        P(("section", "tensor"), "dp", None),
        P("dp", ("section", "tensor"), None, None),
        P(),
    )
    return jax.shard_map(
        shards,
        mesh=mesh,
        in_specs=placed,
        out_specs=(
            P(("section", "tensor"), "dp", None),
            P(("section", "tensor"), "dp", None),
            P(("section", "tensor"), "dp", None),
            P(("section", "tensor"), None, None),
        ),
        check_vma=False,
    )
```

time: 485 us -> 339 us (0.70)
  local copies, waits for them, and re-layouts: 161 us -> 40.2 us
  waiting for transfers between devices: 268 us -> 250 us
  other arithmetic: 17.3 us -> 10.9 us
    scatter x4 -> x0, local copies, waits for them, and re-layouts: 124 us -> none  [the longest x3 118 us: packed(): return empty.at[index].set(values)]
    all_to_all x3, waiting for transfers between devices: 198 us -> 181 us  [move(): lax.all_to_all(values, 'tensor', split_axis=0, concat_axis=0, tiled=True)]
    gather x3 -> x6, local copies, waits for them, and re-layouts: 16.2 us -> 28.3 us  [take(): return values.at[index].get(mode='promise_in_bounds')]
    another operation x7 -> x0, local copies, waits for them, and re-layouts: 8.52 us -> none
    another operation x4 -> x0, other arithmetic: 4.94 us -> none
    unnamed x1 -> x5, local copies, waits for them, and re-layouts: 11.7 us -> 11.7 us
  transfers between devices with their start and end apart: 5 -> 5, of which waited for: 4 -> 4; matrix products, arithmetic and copies ran while one was open for 22% -> 9% of each run, Pallas kernels for 0% -> 0%
where the time goes in v1:
time: 339 us; the launch traced here: 337 us
  waiting for transfers between devices  250 us (74%)
  local copies, waits for them, and re-layouts  40.2 us (12%)
  starting transfers between devices  21.5 us (6%)
  between operations  14.1 us (4%)
  other arithmetic  10.9 us (3%)
    all_to_all x3, waiting for transfers between devices, move(): lax.all_to_all(values, 'tensor', split_axis=0, concat_axis=0, tiled=True)  181 us
    all_gather x1, waiting for transfers between devices, shards(): lax.all_gather(weight_new.astype(jnp.bfloat16), 'dp', axis=1, tiled=True)  68.3 us
    gather x6, local copies, waits for them, and re-layouts, take(): return values.at[index].get(mode='promise_in_bounds')  28.3 us
    all_to_all x3, starting transfers between devices, move(): lax.all_to_all(values, 'tensor', split_axis=0, concat_axis=0, tiled=True)  21.5 us
    unnamed x5, local copies, waits for them, and re-layouts  11.7 us
    convert_element_type x1, other arithmetic, shards(): weight_new.astype(jnp.bfloat16)  9.62 us
  transfers between devices with their start and end apart: 5, of which 4 were waited for; matrix products, arithmetic and copies ran while one was open for 9% of the time, Pallas kernels for 0%

profile of v1, /device:TPU:9, one launch (start us, length us, event | category | flops | bytes accessed | tf_op | source)
XLA Modules:
  0.0 336.9 jit_solution(3969314813310520214)
XLA Ops:
  7.2 0.0 reduce-scatter.2.cloned.1.call-start
  7.2 0.0 copy-start.1
  7.2 0.7 reduce-scatter.2.cloned.1.call-update
  7.9 0.0 copy-done.1
  7.9 0.1 eq.24
  8.1 0.6 convert_reduce_fusion
  8.7 0.1 reshape.72
  8.8 0.1 dynamic-slice_add_fusion
  8.9 0.2 select_reduce_fusion.1
  9.1 4.9 %gather_fusion.4 = bf16[288,32,128]{2,1,0:T(8,128)(2,1)} fusion(f32[288,32,128]{2,1,0:T(8,128)} %param.7, s32[1024]{0:T(1024)S(1)} %pad_clamp_fusion.1), kind=kCustom, calls=%fused_computation.4 | custom fusion | bytes 4719744 | tf_op jit(solution)/shard_map/gather | solution.py:49
  14.0 4.8 %all-to-all-start.2 = ((bf16[288,32,128]{2,1,0:T(8,128)(2,1)}), bf16[288,32,128]{2,1,0:T(8,128)(2,1)S(1)}, u32[]{:S(2)}, u32[]{:S(2)}) async-start(bf16[288,32,128]{2,1,0:T(8,128)(2,1)} %gather_fusion.4), calls=%async_computation.3 | async-start | bytes 4718592 | tf_op jit(solution)/shard_map/all_to_all | solution.py:63
  18.7 5.8 %gather_fusion.2 = bf16[288,32,128]{2,1,0:T(8,128)(2,1)} fusion(f32[288,32,128]{2,1,0:T(8,128)} %param.6, s32[1024]{0:T(1024)S(1)} %pad_clamp_fusion.1), kind=kCustom, calls=%fused_computation.2 | custom fusion | bytes 4719744 | tf_op jit(solution)/shard_map/gather | solution.py:49
  24.5 44.1 %all-to-all-done.2 = bf16[288,32,128]{2,1,0:T(8,128)(2,1)S(1)} async-done(((bf16[288,32,128]{2,1,0:T(8,128)(2,1)}), bf16[288,32,128]{2,1,0:T(8,128)(2,1)S(1)}, u32[]{:S(2)}, u32[]{:S(2)}) %all-to-all-start.2) | async-done | bytes 2359328 | tf_op jit(solution)/shard_map/all_to_all | solution.py:63
  68.7 0.0 copy-start
  68.7 7.9 %all-to-all-start.1 = ((bf16[288,32,128]{2,1,0:T(8,128)(2,1)}), bf16[288,32,128]{2,1,0:T(8,128)(2,1)}, u32[]{:S(2)}, u32[]{:S(2)}) async-start(bf16[288,32,128]{2,1,0:T(8,128)(2,1)} %gather_fusion.2), calls=%async_computation.1 | async-start | bytes 4718592 | tf_op jit(solution)/shard_map/all_to_all | solution.py:63
  76.5 5.4 %gather_fusion = f32[288,32,128]{2,1,0:T(8,128)} fusion(f32[288,32,128]{2,1,0:T(8,128)} %param.5, s32[1024]{0:T(1024)S(1)} %pad_clamp_fusion.1), kind=kCustom, calls=%fused_computation | custom fusion | bytes 9438336 | tf_op jit(solution)/shard_map/gather | solution.py:49
  81.9 0.0 copy-done
  81.9 44.1 %all-to-all-done.1 = bf16[288,32,128]{2,1,0:T(8,128)(2,1)} async-done(((bf16[288,32,128]{2,1,0:T(8,128)(2,1)}), bf16[288,32,128]{2,1,0:T(8,128)(2,1)}, u32[]{:S(2)}, u32[]{:S(2)}) %all-to-all-start.1) | async-done | bytes 2359328 | tf_op jit(solution)/shard_map/all_to_all | solution.py:63
  126.1 8.8 %all-to-all-start = ((f32[288,32,128]{2,1,0:T(8,128)}), f32[288,32,128]{2,1,0:T(8,128)}, u32[]{:S(2)}, u32[]{:S(2)}) async-start(f32[288,32,128]{2,1,0:T(8,128)} %gather_fusion), calls=%async_computation | async-start | bytes 9437184 | tf_op jit(solution)/shard_map/all_to_all | solution.py:63
  134.9 0.0 all-gather.2.cloned.1.call-start
  134.9 0.2 select_reduce_fusion
  135.2 2.8 gather_fusion.5
  138.0 4.1 %gather_fusion.3 = bf16[288,32,128]{2,1,0:T(8,128)(2,1)} fusion(bf16[288,32,128]{2,1,0:T(8,128)(2,1)} %all-to-all-done.1, s32[1024]{0:T(1024)S(1)} %pad_clamp_fusion), kind=kCustom, calls=%fused_computation.3 | custom fusion | bytes 4719744 | tf_op jit(solution)/shard_map/gather | solution.py:49
  142.0 93.0 %all-to-all-done = f32[288,32,128]{2,1,0:T(8,128)} async-done(((f32[288,32,128]{2,1,0:T(8,128)}), f32[288,32,128]{2,1,0:T(8,128)}, u32[]{:S(2)}, u32[]{:S(2)}) %all-to-all-start) | async-done | bytes 4718624 | tf_op jit(solution)/shard_map/all_to_all | solution.py:63
  235.0 5.4 %gather_fusion.1 = f32[288,32,128]{2,1,0:T(8,128)} fusion(f32[288,32,128]{2,1,0:T(8,128)} %all-to-all-done, s32[1024]{0:T(1024)S(1)} %pad_clamp_fusion), kind=kCustom, calls=%fused_computation.1 | custom fusion | bytes 9438336 | tf_op jit(solution)/shard_map/gather | solution.py:49
  240.4 0.0 reduce-scatter.2.cloned.1.call-done
  240.4 9.6 %fusion.12 = (bf16[288,32,128]{2,1,0:T(8,128)(2,1)}, f32[288,32,128]{2,1,0:T(8,128)}, f32[288,32,128]{2,1,0:T(8,128)}, f32[288,32,128]{2,1,0:T(8,128)}) fusion(f32[288,32,128]{2,1,0:T(8,128)} %gather_fusion.1, bf16[288,32,128]{2,1,0:T(8,128)(2,1)} %reduce-scatter.2.cloned.1.call-done, bf16[288,32,128]{2,1,0:T(8,128)(2,1)} %gather_fusion.3, ...), kind=kLoop, calls=%fused_computation.42 | loop fusion | flops 23592960 | bytes 28311552 | tf_op jit(solution)/shard_map/convert_element_type | solution.py:74
  250.0 0.0 all-gather.2.cloned.1.call-update
  250.0 68.3 %all-gather.2.cloned.1.call-done = bf16[288,128,128]{2,1,0:T(8,128)(2,1)} async-done(((bf16[288,32,128]{2,1,0:T(8,128)(2,1)}), bf16[288,128,128]{2,1,0:T(8,128)(2,1)}) %all-gather.2.cloned.1.call-update) | async-done | bytes 9437200 | tf_op jit(solution)/shard_map/all_gather | solution.py:74
  318.3 11.7 %copy.10 = bf16[288,128,128]{2,1,0:T(8,128)(2,1)} copy(bf16[288,128,128]{2,1,0:T(8,128)(2,1)} %all-gather.2.cloned.1.call-done) | data formatting | bytes 18874368
  (7 shorter events, 0.1 us)
Async XLA Ops:
  7.2 233.2 %reduce-scatter.2.cloned.1.call-start = ((), (), s32[]{:S(2)}) async-start(), calls=%async_computation.4 | async-start | bytes 11796480 | tf_op jit(solution)/shard_map/reduce_scatter | solution.py:59
  7.2 0.7 copy-start.1
  14.0 54.7 %all-to-all-start.2 = ((bf16[288,32,128]{2,1,0:T(8,128)(2,1)}), bf16[288,32,128]{2,1,0:T(8,128)(2,1)S(1)}, u32[]{:S(2)}, u32[]{:S(2)}) async-start(bf16[288,32,128]{2,1,0:T(8,128)(2,1)} %gather_fusion.4), calls=%async_computation.3 | async-start | bytes 4718592 | tf_op jit(solution)/shard_map/all_to_all | solution.py:63
  68.7 13.3 %copy-start = (bf16[288,32,128]{2,1,0:T(8,128)(2,1)}, bf16[288,32,128]{2,1,0:T(8,128)(2,1)S(1)}, u32[]{:S(2)}) copy-start(bf16[288,32,128]{2,1,0:T(8,128)(2,1)S(1)} %all-to-all-done.2) | copy-start | bytes 7077892
  68.7 57.4 %all-to-all-start.1 = ((bf16[288,32,128]{2,1,0:T(8,128)(2,1)}), bf16[288,32,128]{2,1,0:T(8,128)(2,1)}, u32[]{:S(2)}, u32[]{:S(2)}) async-start(bf16[288,32,128]{2,1,0:T(8,128)(2,1)} %gather_fusion.2), calls=%async_computation.1 | async-start | bytes 4718592 | tf_op jit(solution)/shard_map/all_to_all | solution.py:63
  126.1 108.9 %all-to-all-start = ((f32[288,32,128]{2,1,0:T(8,128)}), f32[288,32,128]{2,1,0:T(8,128)}, u32[]{:S(2)}, u32[]{:S(2)}) async-start(f32[288,32,128]{2,1,0:T(8,128)} %gather_fusion), calls=%async_computation | async-start | bytes 9437184 | tf_op jit(solution)/shard_map/all_to_all | solution.py:63
  134.9 183.4 %all-gather.2.cloned.1.call-start = ((), (), s32[]{:S(2)}) async-start(), calls=%async_computation.5 | async-start | bytes 11796480 | tf_op jit(solution)/shard_map/all_gather | solution.py:74
Sparse Core Ops, SparseCore 0:
  10.6 78.7 reduce-scatter.1
  250.1 68.1 all-gather.1
